TPU v7x, 32 devices: a whole 2x2x4 slice. The times are simulated.
32 devices in a mesh: vox: 4 (over x, core), var: 8 (over z, y).
Axes of the slice: x: 2, y: 2, z: 4, core: 2. Of those that a mesh axis runs over, the one named last changes fastest.
Arguments:
- cross: float32 [16384, 24576], P('vox', 'var')
- start: float32 [32, 24576], P(None, 'var'), may hold values from -6 to 6
- levels: int32 [2, 32], replicated, may hold values from 0 to 767, as said below
Outputs:
- deflated: float32 [16384, 24576], P('vox', 'var')
- left_dirs: float32 [32, 16384], P(None, 'vox')
- right_dirs: float32 [32, 24576], P(None, 'var')
- strength: float32 [32], replicated
Inputs may be any that keep to these rules, and one draw needn't show every extreme that they name: `levels`: both 0 and 767 occur in every draw.
All inputs are finite; a program needn't handle non-finite values.
Results may differ from a plain program's by a relative error of at most 0.0003.
Values sent between devices are 32-bit elements; how exact they have to be, the bound alone decides.
A program may use at most 192 MiB of HBM per device.

v0:
```python
import math

import jax
import jax.numpy as jnp
from jax import lax
from jax.sharding import PartitionSpec as P

NV = 16384
NG = 24576
ITERS = 2


EPSILON = 1e-06
HIGH = lax.Precision.HIGHEST


def shrink(values, thresholds, mean_sq):
    level = (thresholds * jnp.sqrt(mean_sq + EPSILON))[:, None]
    return values - jnp.clip(values, -level, level)


def local_gram(shrunk):
    return lax.dot_general(
        shrunk, shrunk, (((1,), (1,)), ((), ())), precision=HIGH, preferred_element_type=jnp.float32
    )


def apply_gram(shrunk, gram, count):
    gram = gram / count + EPSILON * jnp.eye(gram.shape[0], dtype=jnp.float32)
    factor = jnp.linalg.cholesky(gram)
    return jax.scipy.linalg.solve_triangular(factor, shrunk, lower=True)


def left_update(cross, right_dirs, thresholds):
    partial_sum = lax.dot_general(
        right_dirs,
        cross,
        (((1,), (1,)), ((), ())),
        precision=HIGH,
        preferred_element_type=jnp.float32,
    )
    summed = lax.psum(partial_sum, "var")
    first_sums = lax.psum(jnp.sum(summed * summed, 1), "vox")
    shrunk = shrink(summed, thresholds, first_sums / NV)
    gram = lax.psum(local_gram(shrunk), "vox")
    return apply_gram(shrunk, gram, NV)


def right_update(cross, left_dirs, thresholds):
    partial_sum = jnp.dot(left_dirs, cross, precision=HIGH, preferred_element_type=jnp.float32)
    summed = lax.psum(partial_sum, "vox")
    first_sums = lax.psum(jnp.sum(summed * summed, 1), "var")
    shrunk = shrink(summed, thresholds, first_sums / NG)
    gram = lax.psum(local_gram(shrunk), "var")
    return apply_gram(shrunk, gram, NG)


def per_device(cross, start, levels):
    thresholds = levels.astype(jnp.float32) / 1024.0
    right_dirs = start
    left_dirs = None
    for sweep in range(ITERS):
        left_dirs = left_update(cross, right_dirs, thresholds[0])
        right_dirs = right_update(cross, left_dirs, thresholds[1])
    projected = lax.dot_general(
        right_dirs,
        cross,
        (((1,), (1,)), ((), ())),
        precision=HIGH,
        preferred_element_type=jnp.float32,
    )
    strength = lax.psum(jnp.sum(left_dirs * projected, 1), ("vox", "var")) / math.sqrt(NV * NG)
    scaled = left_dirs * (strength / math.sqrt(NV * NG))[:, None]
    removed = lax.dot_general(
        scaled,
        right_dirs,
        (((0,), (0,)), ((), ())),
        precision=HIGH,
        preferred_element_type=jnp.float32,
    )
    deflated = cross - removed
    return (deflated, left_dirs, right_dirs, strength)


def solution(mesh):
    in_specs = (P("vox", "var"), P(None, "var"), P())
    out_specs = (P("vox", "var"), P(None, "vox"), P(None, "var"), P())
    return jax.shard_map(
        per_device, mesh=mesh, in_specs=in_specs, out_specs=out_specs, check_vma=False
    )
```

profile of v0, /device:TPU:0, one launch (start us, length us, event | category | flops | bytes accessed | tf_op | source)
XLA Modules:
  0.0 712.8 jit_solution(12268424818224196377)
XLA Ops:
  7.2 0.9 copy-done
  8.2 49.4 %fusion.47 = f32[32,4096]{1,0:T(8,128)} fusion(f32[32,3072]{1,0:T(8,128)S(1)} %copy-done, f32[4096,3072]{1,0:T(8,128)} %param.8), kind=kOutput, calls=%fused_computation.85 | convolution fusion | flops 4831838208 | bytes 51249152 | tf_op jit(solution)/shard_map/dot_general | solution.py:35
  57.7 75.5 %all-reduce.5.cloned.1.call-done = f32[32,4096]{1,0:T(8,128)} async-done(((f32[32,4096]{1,0:T(8,128)}), f32[32,4096]{1,0:T(8,128)}) %all-reduce.5.cloned.1.call-update) | async-done | bytes 524304 | tf_op jit(solution)/shard_map/psum | solution.py:42
  133.2 1.2 multiply_reduce_fusion.1
  134.4 5.7 psum.92
  140.1 1.9 fusion.3
  142.0 11.2 %psum.93 = f32[32,32]{0,1:T(8,128)S(1)} all-reduce(f32[32,32]{0,1:T(8,128)S(1)} %fusion.3), channel_id=1, replica_groups=mesh['vox'=4,'var'=8] {'vox'}, use_global_device_ids=true, to_apply=%region_3.4 | all-reduce | flops 1024 | bytes 8192 | tf_op jit(solution)/shard_map/psum | solution.py:45
  153.3 2.9 cholesky.74
  156.3 0.6 compare_reduce_fusion.3
  156.9 0.7 fusion.27
  157.6 2.4 custom-call.10
  160.0 1.7 fusion.2
  161.7 34.2 %fusion.48 = f32[32,3072]{1,0:T(8,128)} fusion(f32[32,4096]{1,0:T(8,128)S(1)} %fusion.2, f32[4096,3072]{1,0:T(8,128)} %param.8), kind=kOutput, calls=%fused_computation.86 | convolution fusion | flops 4831838208 | bytes 51249152 | tf_op jit(solution)/shard_map/dot_general | solution.py:50
  196.0 31.5 %all-reduce.7.cloned.1.call-done = f32[32,3072]{1,0:T(8,128)} async-done(((f32[32,3072]{1,0:T(8,128)}), f32[32,3072]{1,0:T(8,128)}) %all-reduce.7.cloned.1.call-update) | async-done | bytes 393232 | tf_op jit(solution)/shard_map/psum | solution.py:51
  227.6 1.1 multiply_reduce_fusion.3
  228.7 21.4 %psum.95 = f32[32]{0:T(128)S(1)} all-reduce(f32[32]{0:T(128)S(1)} %multiply_reduce_fusion.3), channel_id=1, replica_groups=mesh['vox'=4,'var'=8] {'var'}, use_global_device_ids=true, to_apply=%region_8.11 | all-reduce | flops 32 | bytes 256 | tf_op jit(solution)/shard_map/psum | solution.py:52
  250.1 1.7 fusion.7
  251.8 33.2 %psum.96 = f32[32,32]{0,1:T(8,128)S(1)} all-reduce(f32[32,32]{0,1:T(8,128)S(1)} %fusion.7), channel_id=1, replica_groups=mesh['vox'=4,'var'=8] {'var'}, use_global_device_ids=true, to_apply=%region_9.12 | all-reduce | flops 1024 | bytes 8192 | tf_op jit(solution)/shard_map/psum | solution.py:54
  285.1 2.9 cholesky.85
  288.1 0.6 compare_reduce_fusion.2
  288.7 0.7 fusion.28
  289.4 2.4 custom-call.11
  291.8 1.6 fusion.6
  293.4 49.4 %fusion.49 = f32[32,4096]{1,0:T(8,128)} fusion(f32[32,3072]{1,0:T(8,128)S(1)} %fusion.6, f32[4096,3072]{1,0:T(8,128)} %param.8), kind=kOutput, calls=%fused_computation.87 | convolution fusion | flops 4831838208 | bytes 51249152 | tf_op jit(solution)/shard_map/dot_general | solution.py:35
  342.9 69.1 %all-reduce.9.cloned.1.call-done = f32[32,4096]{1,0:T(8,128)} async-done(((f32[32,4096]{1,0:T(8,128)}), f32[32,4096]{1,0:T(8,128)}) %all-reduce.9.cloned.1.call-update) | async-done | bytes 524304 | tf_op jit(solution)/shard_map/psum | solution.py:42
  412.0 1.2 multiply_reduce_fusion
  413.1 5.7 psum.98
  418.8 1.9 fusion.5
  420.8 11.5 %psum.99 = f32[32,32]{0,1:T(8,128)S(1)} all-reduce(f32[32,32]{0,1:T(8,128)S(1)} %fusion.5), channel_id=1, replica_groups=mesh['vox'=4,'var'=8] {'vox'}, use_global_device_ids=true, to_apply=%region_13.17 | all-reduce | flops 1024 | bytes 8192 | tf_op jit(solution)/shard_map/psum | solution.py:45
  432.3 2.9 cholesky.96
  435.3 0.6 compare_reduce_fusion.1
  435.9 0.7 fusion.29
  436.6 2.4 custom-call.12
  439.0 1.7 fusion.4
  440.8 34.4 %fusion.50 = f32[32,3072]{1,0:T(8,128)} fusion(f32[32,4096]{1,0:T(8,128)S(1)} %fusion.4, f32[4096,3072]{1,0:T(8,128)} %param.8), kind=kOutput, calls=%fused_computation.88 | convolution fusion | flops 4831838208 | bytes 51249152 | tf_op jit(solution)/shard_map/dot_general | solution.py:50
  475.2 31.6 %all-reduce.11.cloned.1.call-done = f32[32,3072]{1,0:T(8,128)} async-done(((f32[32,3072]{1,0:T(8,128)}), f32[32,3072]{1,0:T(8,128)}) %all-reduce.11.cloned.1.call-update) | async-done | bytes 393232 | tf_op jit(solution)/shard_map/psum | solution.py:51
  506.8 1.1 multiply_reduce_fusion.2
  507.9 21.4 %psum.101 = f32[32]{0:T(128)S(1)} all-reduce(f32[32]{0:T(128)S(1)} %multiply_reduce_fusion.2), channel_id=1, replica_groups=mesh['vox'=4,'var'=8] {'var'}, use_global_device_ids=true, to_apply=%region_16.20 | all-reduce | flops 32 | bytes 256 | tf_op jit(solution)/shard_map/psum | solution.py:52
  529.3 1.7 fusion.9
  531.0 33.2 %psum.102 = f32[32,32]{0,1:T(8,128)S(1)} all-reduce(f32[32,32]{0,1:T(8,128)S(1)} %fusion.9), channel_id=1, replica_groups=mesh['vox'=4,'var'=8] {'var'}, use_global_device_ids=true, to_apply=%region_17.21 | all-reduce | flops 1024 | bytes 8192 | tf_op jit(solution)/shard_map/psum | solution.py:54
  564.3 2.9 cholesky.107
  567.2 0.6 compare_reduce_fusion
  567.8 0.7 fusion.30
  568.5 2.4 custom-call.13
  570.9 1.6 fusion.8
  572.5 48.9 %fusion = f32[32]{0:T(128)S(1)} fusion(f32[32,4096]{1,0:T(8,128)S(1)} %fusion.4, f32[32,3072]{1,0:T(8,128)S(1)} %fusion.8, f32[4096,3072]{1,0:T(8,128)} %param.8), kind=kOutput, calls=%fused_computation.2 | convolution fusion | flops 4832100352 | bytes 51249280 | tf_op jit(solution)/shard_map/dot_general | solution.py:65
  621.4 37.1 %psum.103 = f32[32]{0:T(128)S(1)} all-reduce(f32[32]{0:T(128)S(1)} %fusion), channel_id=1, replica_groups=mesh['vox'=4,'var'=8] {'vox','var'}, use_global_device_ids=true, to_apply=%region_19.23 | all-reduce | flops 32 | bytes 256 | tf_op jit(solution)/shard_map/psum | solution.py:72
  659.0 47.0 %convolution_subtract_fusion = f32[4096,3072]{1,0:T(8,128)} fusion(f32[4096,3072]{1,0:T(8,128)} %param.8, f32[32,3072]{1,0:T(8,128)S(1)} %fusion.8, f32[32,4096]{1,0:T(8,128)S(1)} %fusion.4, f32[32]{0:T(128)S(1)} %get-tuple-element.16), kind=kOutput, calls=%fused_computation | convolution fusion | flops 4844552192 | bytes 101580928 | tf_op jit(solution)/shard_map/dot_general | solution.py:74
  (39 shorter events, 1.3 us)
Async XLA Ops:
  7.2 1.0 copy-start
  7.2 50.5 %copy-start.4 = (s32[2,32]{1,0:T(2,128)S(1)}, s32[2,32]{1,0:T(2,128)}, u32[]{:S(2)}) copy-start(s32[2,32]{1,0:T(2,128)} %param.10) | copy-start | bytes 772
  7.2 126.0 %all-reduce.5.cloned.1.call-start = ((), (), s32[]{:S(2)}) async-start(), calls=%async_computation | async-start | bytes 1048576 | tf_op jit(solution)/shard_map/psum | solution.py:42
  57.6 170.0 %all-reduce.7.cloned.1.call-start = ((), (), s32[]{:S(2)}) async-start(), calls=%async_computation.1 | async-start | bytes 786432 | tf_op jit(solution)/shard_map/psum | solution.py:51
  196.0 216.0 %all-reduce.9.cloned.1.call-start = ((), (), s32[]{:S(2)}) async-start(), calls=%async_computation.2 | async-start | bytes 1048576 | tf_op jit(solution)/shard_map/psum | solution.py:42
  342.8 163.9 %all-reduce.11.cloned.1.call-start = ((), (), s32[]{:S(2)}) async-start(), calls=%async_computation.3 | async-start | bytes 786432 | tf_op jit(solution)/shard_map/psum | solution.py:51
  440.7 218.3 %copy-start.2 = (f32[32,4096]{1,0:T(8,128)}, f32[32,4096]{1,0:T(8,128)S(1)}, u32[]{:S(2)}) copy-start(f32[32,4096]{1,0:T(8,128)S(1)} %fusion.4) | copy-start | bytes 1572868
  572.5 133.5 %copy-start.3 = (f32[32,3072]{1,0:T(8,128)}, f32[32,3072]{1,0:T(8,128)S(1)}, u32[]{:S(2)}) copy-start(f32[32,3072]{1,0:T(8,128)S(1)} %fusion.8) | copy-start | bytes 1179652
  659.0 47.0 %copy-start.1 = (f32[32,3072]{1,0:T(8,128)S(1)}, f32[32,3072]{1,0:T(8,128)}, u32[]{:S(2)}) copy-start(f32[32,3072]{1,0:T(8,128)} %param.9) | copy-start | bytes 1179652
Sparse Core Ops, SparseCore 0:
  57.7 75.4 all-reduce.4
  196.1 31.4 all-reduce.6
  343.0 68.9 all-reduce.8
  475.3 31.4 all-reduce.10
where the time goes:
time: 720 us; the launch traced here: 713 us
  matrix products  277 us (38%)
  waiting for transfers between devices  208 us (29%)
  blocking collectives  180 us (25%)
  other arithmetic  32 us (4%)
  between operations  14.2 us (2%)
    psum x2, waiting for transfers between devices, left_update(): summed = lax.psum(partial_sum, 'var')  145 us
    dot_general x2, matrix products, left_update(): lax.dot_general(right_dirs, cross, (((1,), (1,)), ((), ())), precision=HI...  98.8 us
    dot_general x2, matrix products, right_update(): jnp.dot(left_dirs, cross, precision=HIGH, preferred_element_type=jnp.floa...  68.6 us
    psum x2, blocking collectives, right_update(): gram = lax.psum(local_gram(shrunk), 'var')  66.4 us
    psum x2, waiting for transfers between devices, right_update(): summed = lax.psum(partial_sum, 'vox')  63.1 us
    dot_general x1, matrix products, per_device(): lax.dot_general(right_dirs, cross, (((1,), (1,)), ((), ())), precision=HI...  48.9 us
    dot_general x1, matrix products, per_device(): lax.dot_general(scaled, right_dirs, (((0,), (0,)), ((), ())), precision=H...  47 us
    psum x2, blocking collectives, right_update(): first_sums = lax.psum(jnp.sum(summed * summed, 1), 'var')  42.7 us
  transfers between devices with their start and end apart: 4, of which 4 were waited for; matrix products, arithmetic and copies ran while one was open for 0% of the time, Pallas kernels for 0%

commit v1 on v0

v1 whole, which is shorter than its diff:
```python
import functools
import math

import jax
import jax.numpy as jnp
from jax import lax
from jax.experimental import pallas as pl
from jax.experimental.pallas import tpu as pltpu
from jax.sharding import PartitionSpec as P

ITERS = 2
EPSILON = 1e-06
HIGH = lax.Precision.HIGHEST
MESH = pl.DeviceIdType.MESH
F32 = jnp.float32
BF16 = jnp.bfloat16
LANES = 128
ROWS = 512
COLUMNS = 384


def halves(values):
    high = values.astype(BF16)
    return high, (values - high.astype(F32)).astype(BF16)


def block_rows(rows):
    return math.gcd(rows, ROWS)


def left_kernel(chunk, dirs_ref, cross_ref, out_ref, stacked):
    k = dirs_ref.shape[0]

    @pl.when(pl.program_id(0) == 0)
    def _():
        high, low = halves(dirs_ref[...])
        stacked[:k, :] = high
        stacked[k:, :] = low

    high, low = halves(cross_ref[...])
    dims = (((1,), (1,)), ((), ()))
    total = lax.dot_general(high, stacked[...], dims, preferred_element_type=F32)
    total = total + lax.dot_general(low, stacked[...], dims, preferred_element_type=F32)
    total = total.T
    total = total[:k] + total[k:]
    for at in range(out_ref.shape[0]):
        out_ref[at] = total[:, at * chunk : (at + 1) * chunk]


def left_pass(cross, dirs, chunk):
    rows, cols = cross.shape
    k = dirs.shape[0]
    size = block_rows(rows)
    size = max(size, chunk)
    return pl.pallas_call(
        functools.partial(left_kernel, chunk),
        out_shape=jax.ShapeDtypeStruct((rows // chunk, k, chunk), F32),
        grid=(rows // size,),
        in_specs=[
            pl.BlockSpec((k, cols), lambda i: (0, 0)),
            pl.BlockSpec((size, cols), lambda i: (i, 0)),
        ],
        out_specs=pl.BlockSpec((size // chunk, k, chunk), lambda i: (i, 0, 0)),
        scratch_shapes=[pltpu.VMEM((2 * k, cols), BF16)],
        name="left_pass",
    )(dirs, cross)


def right_kernel(dirs_ref, cross_ref, out_ref, stacked):
    k = dirs_ref.shape[0]

    @pl.when(pl.program_id(0) == 0)
    def _():
        high, low = halves(dirs_ref[...])
        stacked[:k, :] = high
        stacked[k:, :] = low

    high, low = halves(cross_ref[...])
    total = jnp.dot(stacked[...], high, preferred_element_type=F32)
    total = total + jnp.dot(stacked[...], low, preferred_element_type=F32)
    out_ref[0] = total[:k] + total[k:]


def right_pass(cross, dirs, chunk):
    rows, cols = cross.shape
    k = dirs.shape[0]
    size = math.gcd(chunk, COLUMNS)
    per = chunk // size
    return pl.pallas_call(
        right_kernel,
        out_shape=jax.ShapeDtypeStruct((cols // chunk, k, chunk), F32),
        grid=(cols // size,),
        in_specs=[
            pl.BlockSpec((k, rows), lambda j: (0, 0)),
            pl.BlockSpec((rows, size), lambda j: (0, j)),
        ],
        out_specs=pl.BlockSpec((1, k, size), lambda j: (j // per, 0, j % per)),
        scratch_shapes=[pltpu.VMEM((2 * k, rows), BF16)],
        name="right_pass",
    )(dirs, cross)


def deflate_kernel(left_ref, scale_ref, right_ref, cross_ref, out_ref, stacked):
    k = right_ref.shape[0]

    @pl.when(pl.program_id(0) == 0)
    def _():
        high, low = halves(right_ref[...])
        stacked[:k, :] = high
        stacked[k : 2 * k, :] = high
        stacked[2 * k :, :] = low

    high, low = halves(left_ref[...] * scale_ref[:, :1])
    scaled = jnp.concatenate([high, low, high], axis=0)
    removed = lax.dot_general(
        scaled, stacked[...], (((0,), (0,)), ((), ())), preferred_element_type=F32
    )
    out_ref[...] = cross_ref[...] - removed


def deflate(cross, left_dirs, scale, right_dirs):
    rows, cols = cross.shape
    k = left_dirs.shape[0]
    size = block_rows(rows)
    return pl.pallas_call(
        deflate_kernel,
        out_shape=jax.ShapeDtypeStruct((rows, cols), F32),
        grid=(rows // size,),
        in_specs=[
            pl.BlockSpec((k, size), lambda i: (0, i)),
            pl.BlockSpec((k, LANES), lambda i: (0, 0)),
            pl.BlockSpec((k, cols), lambda i: (0, 0)),
            pl.BlockSpec((size, cols), lambda i: (i, 0)),
        ],
        out_specs=pl.BlockSpec((size, cols), lambda i: (i, 0)),
        scratch_shapes=[pltpu.VMEM((3 * k, cols), BF16)],
        name="deflate",
    )(left_dirs, scale, right_dirs, cross)


def inverse_factor(gram):
    k = gram.shape[0]
    row = lax.broadcasted_iota(jnp.int32, gram.shape, 0)
    lane = lax.broadcasted_iota(jnp.int32, gram.shape, 1)
    table = jnp.where(lane < k, gram, jnp.where(lane == row + k, 1.0, 0.0))
    below = row[:, :1]
    for at in range(k - 1):
        pivot = table[at : at + 1, :]
        column = table[:, at : at + 1]
        factor = jnp.where(below > at, column / pivot[:, at : at + 1], 0.0)
        table = table - factor * pivot
    diag = jnp.sum(jnp.where(lane == row, table, 0.0), axis=1, keepdims=True)
    return pltpu.roll(table / jnp.sqrt(diag), LANES - k, 1)[:, :k]


def pack(table):
    k = table.shape[0]
    rows = k * k // LANES
    group = lax.broadcasted_iota(jnp.int32, (rows, LANES), 1) // k
    packed = table[:rows]
    for at in range(1, LANES // k):
        packed = jnp.where(group == at, table[at * rows : (at + 1) * rows], packed)
    return packed


def unpack(packed, k):
    pieces = [packed]
    for at in range(1, LANES // k):
        pieces.append(pltpu.roll(packed, LANES - at * k, 1))
    return jnp.concatenate(pieces, axis=0)


def exchange(table, count, axis, me, sends, recvs):
    copies = []
    for hop in range(1, count):
        other = lax.rem(me + hop, count)
        copy = pltpu.make_async_remote_copy(
            src_ref=table.at[me],
            dst_ref=table.at[me],
            send_sem=sends.at[hop - 1],
            recv_sem=recvs.at[hop - 1],
            device_id={axis: other},
            device_id_type=MESH,
        )
        copy.start()
        copies.append(copy)
    return copies


def orth_kernel(axis, parts, other_axis, others, count, final, part_ref, thr_ref, *refs):
    outs, refs = refs[: 2 if final else 1], refs[2 if final else 1 :]
    landed, gathered, squares, grams, rs_s, rs_r, ag_s, ag_r, sq_s, sq_r, gr_s, gr_r = refs
    dirs_ref = outs[0]
    pieces, k, chunk = part_ref.shape
    me = lax.axis_index(axis)
    mine = lax.axis_index(other_axis)

    barrier = pltpu.get_barrier_semaphore()
    for hop in range(1, parts):
        pl.semaphore_signal(
            barrier, inc=1, device_id={axis: lax.rem(me + hop, parts)}, device_id_type=MESH
        )
    for hop in range(1, others):
        pl.semaphore_signal(
            barrier, inc=1, device_id={other_axis: lax.rem(mine + hop, others)}, device_id_type=MESH
        )
    pl.semaphore_wait(barrier, parts + others - 2)

    if parts > 1:
        first = []
        for hop in range(1, parts):
            other = lax.rem(me + hop, parts)
            copy = pltpu.make_async_remote_copy(
                src_ref=part_ref.at[other],
                dst_ref=landed.at[hop - 1],
                send_sem=rs_s.at[hop - 1],
                recv_sem=rs_r.at[hop - 1],
                device_id={axis: other},
                device_id_type=MESH,
            )
            copy.start()
            first.append(copy)
        total = part_ref[me]
        for hop in range(1, parts):
            first[hop - 1].wait()
            total = total + landed[hop - 1]
        gathered[me] = total
        for copy in exchange(gathered, parts, axis, me, ag_s, ag_r):
            copy.wait()
    else:
        gathered[...] = part_ref[...]

    sums = jnp.zeros((k, chunk), F32)
    for at in range(pieces):
        values = gathered[at]
        sums = sums + values * values
    squares[mine] = pack(jnp.broadcast_to(jnp.sum(sums, axis=1, keepdims=True), (k, LANES)))
    for copy in exchange(squares, others, other_axis, mine, sq_s, sq_r):
        copy.wait()
    mean = squares[0]
    for at in range(1, others):
        mean = mean + squares[at]
    mean = unpack(mean, k)
    level = (thr_ref[...] * jnp.sqrt(mean / count + EPSILON))[:, :1]

    gram = jnp.zeros((2 * k if final else k, LANES), F32)
    shrunk = []
    for at in range(pieces):
        values = gathered[at]
        short = values - jnp.clip(values, -level, level)
        shrunk.append(short)
        against = jnp.concatenate([short] * (LANES // k), axis=0)
        rows = jnp.concatenate([short, values], axis=0) if final else short
        gram = gram + lax.dot_general(
            rows, against, (((1,), (1,)), ((), ())), precision=HIGH, preferred_element_type=F32
        )
    half = squares.shape[1]
    if final:
        grams[mine] = jnp.concatenate([pack(gram[:k]), pack(gram[k:])], axis=0)
    else:
        grams[mine] = pack(gram)
    for copy in exchange(grams, others, other_axis, mine, gr_s, gr_r):
        copy.wait()
    gram = grams[0]
    for at in range(1, others):
        gram = gram + grams[at]
    cross_gram = unpack(gram[half:], k) if final else None
    gram = unpack(gram[:half], k)
    row = lax.broadcasted_iota(jnp.int32, (k, LANES), 0)
    lane = lax.broadcasted_iota(jnp.int32, (k, LANES), 1)
    inverse = inverse_factor(gram / count + jnp.where(row == lane, EPSILON, 0.0))
    for at in range(pieces):
        dirs_ref[:, at * chunk : (at + 1) * chunk] = jnp.dot(
            inverse, shrunk[at], precision=HIGH, preferred_element_type=F32
        )
    if final:
        strength = jnp.sum(cross_gram[:, :k] * inverse, axis=1, keepdims=True)
        outs[1][...] = jnp.broadcast_to(strength, (k, LANES))


def orth_step(partial, thresholds, axis, parts, other_axis, others, count, ident, final=False):
    pieces, k, chunk = partial.shape
    if pieces != parts:
        partial = lax.psum(partial, axis)
        parts = 1
    slots = max(parts - 1, 1)
    dma = pltpu.SemaphoreType.DMA
    vmem = pl.BlockSpec(memory_space=pltpu.VMEM)
    out_shape = [jax.ShapeDtypeStruct((k, pieces * chunk), F32)]
    if final:
        out_shape.append(jax.ShapeDtypeStruct((k, LANES), F32))
    return pl.pallas_call(
        functools.partial(orth_kernel, axis, parts, other_axis, others, count, final),
        out_shape=out_shape,
        in_specs=[vmem, vmem],
        out_specs=[vmem] * len(out_shape),
        scratch_shapes=[
            pltpu.VMEM((slots, k, chunk), F32),
            pltpu.VMEM((pieces, k, chunk), F32),
            pltpu.VMEM((others, k * k // LANES, LANES), F32),
            pltpu.VMEM((others, (2 if final else 1) * k * k // LANES, LANES), F32),
            dma((slots,)),
            dma((slots,)),
            dma((slots,)),
            dma((slots,)),
            dma((others - 1,)),
            dma((others - 1,)),
            dma((others - 1,)),
            dma((others - 1,)),
        ],
        compiler_params=pltpu.CompilerParams(collective_id=ident, has_side_effects=True),
        name=f"orth_{ident}",
    )(partial, thresholds)


def chunk_of(size, parts):
    chunk = size // parts
    return chunk if chunk * parts == size and chunk % LANES == 0 else size


def solution(mesh):
    vox, var = mesh.shape["vox"], mesh.shape["var"]

    def per_device(cross, start, levels):
        rows, cols = cross.shape
        k = start.shape[0]
        nv, ng = rows * vox, cols * var
        thresholds = levels.astype(F32) / 1024.0
        thresholds = jnp.broadcast_to(thresholds[:, :, None], (2, k, LANES))
        row_chunk, col_chunk = chunk_of(rows, var), chunk_of(cols, vox)
        right_dirs = start
        for sweep in range(ITERS):
            final = sweep == ITERS - 1
            partial = left_pass(cross, right_dirs, row_chunk)
            left_dirs = orth_step(partial, thresholds[0], "var", var, "vox", vox, nv, 2 * sweep)[0]
            partial = right_pass(cross, left_dirs, col_chunk)
            outs = orth_step(
                partial, thresholds[1], "vox", vox, "var", var, ng, 2 * sweep + 1, final
            )
            right_dirs = outs[0]
        root = math.sqrt(nv * ng)
        strength = outs[1] / root
        deflated = deflate(cross, left_dirs, strength / root, right_dirs)
        return (deflated, left_dirs, right_dirs, strength[:, 0])

    in_specs = (P("vox", "var"), P(None, "var"), P())
    out_specs = (P("vox", "var"), P(None, "vox"), P(None, "var"), P())
    return jax.shard_map(
        per_device, mesh=mesh, in_specs=in_specs, out_specs=out_specs, check_vma=False
    )
```

time: 720 us -> 268 us (0.37)
  matrix products: 277 us -> 0 us
  Pallas kernels: 0 us -> 260 us
  waiting for transfers between devices: 208 us -> 0 us
  blocking collectives: 180 us -> 0 us
  other arithmetic: 32 us -> 2.63 us
  between operations: 14.2 us -> 0.67 us
    dot_general x10 -> x0, matrix products: 271 us -> none  [the longest x2 98.8 us: left_update(): lax.dot_general(right_dirs, cross, (((1,), (1,)), ((), ())), precision=HI...]
    pallas_call x0 -> x9, Pallas kernels: none -> 260 us  [the longest x4 144 us: orth_step(): pl.pallas_call(functools.partial(orth_kernel, axis, parts, other_axis, ot...]
    psum x4 -> x0, waiting for transfers between devices: 208 us -> none  [the longest x2 145 us: left_update(): summed = lax.psum(partial_sum, 'var')]
    psum x9 -> x0, blocking collectives: 180 us -> none  [the longest x2 66.4 us: right_update(): gram = lax.psum(local_gram(shrunk), 'var')]
    another operation x20 -> x0, other arithmetic: 26.7 us -> none  [the longest x12 14.4 us: apply_gram(): factor = jnp.linalg.cholesky(gram)]
  transfers between devices with their start and end apart: 4 -> 0, of which waited for: 4 -> 0; matrix products, arithmetic and copies ran while one was open for 0% -> 0% of each run, Pallas kernels for 0% -> 0%
where the time goes in v1:
time: 268 us; the launch traced here: 267 us
  Pallas kernels  260 us (97%)
  local copies, waits for them, and re-layouts  2.9 us (1%)
    pallas_call x4, Pallas kernels, orth_step(): pl.pallas_call(functools.partial(orth_kernel, axis, parts, other_axis, ot...  144 us
    pallas_call x2, Pallas kernels, left_pass(): pl.pallas_call(functools.partial(left_kernel, chunk), out_shape=jax.Shape...  43.4 us
    pallas_call x2, Pallas kernels, right_pass(): pl.pallas_call(right_kernel, out_shape=jax.ShapeDtypeStruct((cols // chun...  39.4 us
    pallas_call x1, Pallas kernels, deflate(): pl.pallas_call(deflate_kernel, out_shape=jax.ShapeDtypeStruct((rows, cols...  34.1 us

profile of v1, /device:TPU:0, one launch (start us, length us, event | category | flops | bytes accessed | tf_op | source)
XLA Modules:
  0.0 266.6 jit_solution(14833241213674349370)
XLA Ops:
  0.6 0.7 convert_multiply_fusion
  1.3 0.7 broadcast_in_dim.13.thr_ref
  2.0 21.7 %left_pass.2.part_ref = f32[8,32,512]{2,1,0:T(8,128)} custom-call(f32[32,3072]{1,0:T(8,128)} %dirs_ref.1, f32[4096,3072]{1,0:T(8,128)} %cross_ref.9), custom_call_target="tpu_custom_call" | custom-call | tf_op jit(solution)/shard_map/left_pass/pallas_call | solution.py:55
  23.7 40.9 %orth_0.1.dirs_ref = f32[32,4096]{1,0:T(8,128)} custom-call(f32[8,32,512]{2,1,0:T(8,128)} %left_pass.2.part_ref, f32[32,128]{1,0:T(8,128)} %broadcast_in_dim.13.thr_ref), custom_call_target="tpu_custom_call" | custom-call | tf_op jit(solution)/shard_map/orth_0/pallas_call | solution.py:292
  64.6 19.7 %right_pass.2.part_ref = f32[4,32,768]{2,1,0:T(8,128)} custom-call(f32[32,4096]{1,0:T(8,128)} %orth_0.1.dirs_ref, f32[4096,3072]{1,0:T(8,128)} %cross_ref.9), custom_call_target="tpu_custom_call" | custom-call | tf_op jit(solution)/shard_map/right_pass/pallas_call | solution.py:89
  84.3 0.7 broadcast_in_dim.15.thr_ref
  85.0 34.0 %orth_1.1.dirs_ref = f32[32,3072]{1,0:T(8,128)} custom-call(f32[4,32,768]{2,1,0:T(8,128)} %right_pass.2.part_ref, f32[32,128]{1,0:T(8,128)} %broadcast_in_dim.15.thr_ref), custom_call_target="tpu_custom_call" | custom-call | tf_op jit(solution)/shard_map/orth_1/pallas_call | solution.py:292
  119.0 21.7 %left_pass.3.part_ref = f32[8,32,512]{2,1,0:T(8,128)} custom-call(f32[32,3072]{1,0:T(8,128)} %orth_1.1.dirs_ref, f32[4096,3072]{1,0:T(8,128)} %cross_ref.9), custom_call_target="tpu_custom_call" | custom-call | tf_op jit(solution)/shard_map/left_pass/pallas_call | solution.py:55
  140.7 38.1 %orth_2.1.dirs_ref.left_ref = f32[32,4096]{1,0:T(8,128)} custom-call(f32[8,32,512]{2,1,0:T(8,128)} %left_pass.3.part_ref, f32[32,128]{1,0:T(8,128)} %broadcast_in_dim.13.thr_ref), custom_call_target="tpu_custom_call" | custom-call | tf_op jit(solution)/shard_map/orth_2/pallas_call | solution.py:292
  178.8 19.7 %right_pass.3.part_ref = f32[4,32,768]{2,1,0:T(8,128)} custom-call(f32[32,4096]{1,0:T(8,128)} %orth_2.1.dirs_ref.left_ref, f32[4096,3072]{1,0:T(8,128)} %cross_ref.9), custom_call_target="tpu_custom_call" | custom-call | tf_op jit(solution)/shard_map/right_pass/pallas_call | solution.py:89
  198.5 30.5 %orth_3.1 = (f32[32,3072]{1,0:T(8,128)}, f32[32,128]{1,0:T(8,128)}) custom-call(f32[4,32,768]{2,1,0:T(8,128)} %right_pass.3.part_ref, f32[32,128]{1,0:T(8,128)} %broadcast_in_dim.15.thr_ref), custom_call_target="tpu_custom_call" | custom-call | tf_op jit(solution)/shard_map/orth_3/pallas_call | solution.py:292
  229.0 1.3 broadcast_multiply_fusion.scale_ref
  230.3 0.0 copy-start.2
  230.3 0.0 copy-start
  230.3 0.0 copy-start.1
  230.3 34.1 %deflate.1 = f32[4096,3072]{1,0:T(8,128)} custom-call(f32[32,4096]{1,0:T(8,128)} %orth_2.1.dirs_ref.left_ref, f32[32,128]{1,0:T(8,128)} %broadcast_multiply_fusion.scale_ref, f32[32,3072]{1,0:T(8,128)} %get-tuple-element.16.right_ref, f32[4096,3072]{1,0:T(8,128)} %cross_ref.9), custom_call_target="tpu_custom_call" | custom-call | tf_op jit(solution)/shard_map/deflate/pallas_call | solution.py:125
  264.4 0.0 copy-done.2
  264.4 0.6 fusion
  265.1 0.0 copy-done
  265.1 0.8 copy.9
  265.9 0.0 copy-done.1
  265.9 0.7 copy.10
  (1 shorter events, 0.0 us)
Async XLA Ops:
  230.3 34.1 %copy-start.2 = (f32[32,128]{1,0:T(8,128)S(1)}, f32[32,128]{1,0:T(8,128)}, u32[]{:S(2)}) copy-start(f32[32,128]{1,0:T(8,128)} %get-tuple-element.6) | copy-start | bytes 49156
  230.3 34.8 %copy-start = (f32[32,4096]{1,0:T(8,128)S(1)}, f32[32,4096]{1,0:T(8,128)}, u32[]{:S(2)}) copy-start(f32[32,4096]{1,0:T(8,128)} %orth_2.1.dirs_ref.left_ref) | copy-start | bytes 1572868
  230.3 35.5 %copy-start.1 = (f32[32,3072]{1,0:T(8,128)S(1)}, f32[32,3072]{1,0:T(8,128)}, u32[]{:S(2)}) copy-start(f32[32,3072]{1,0:T(8,128)} %get-tuple-element.16.right_ref) | copy-start | bytes 1179652

commit v2 on v1

--- a/solution.py
+++ b/solution.py
@@ -10,7 +10,6 @@
 
 ITERS = 2
 EPSILON = 1e-06
-HIGH = lax.Precision.HIGHEST
 MESH = pl.DeviceIdType.MESH
 F32 = jnp.float32
 BF16 = jnp.bfloat16
@@ -243,17 +242,25 @@
     mean = unpack(mean, k)
     level = (thr_ref[...] * jnp.sqrt(mean / count + EPSILON))[:, :1]
 
-    gram = jnp.zeros((2 * k if final else k, LANES), F32)
+    gram = jnp.zeros((2 * k if final else k, k), F32)
     shrunk = []
+    dims = (((1,), (1,)), ((), ()))
     for at in range(pieces):
         values = gathered[at]
-        short = values - jnp.clip(values, -level, level)
-        shrunk.append(short)
-        against = jnp.concatenate([short] * (LANES // k), axis=0)
-        rows = jnp.concatenate([short, values], axis=0) if final else short
-        gram = gram + lax.dot_general(
-            rows, against, (((1,), (1,)), ((), ())), precision=HIGH, preferred_element_type=F32
-        )
+        high, low = halves(values - jnp.clip(values, -level, level))
+        shrunk.append((high, low))
+        rows = [high, low]
+        tops = high
+        if final:
+            rows += list(halves(values))
+            tops = jnp.concatenate([high, rows[2]], axis=0)
+        rows = jnp.concatenate(rows, axis=0)
+        wide = lax.dot_general(rows, high, dims, preferred_element_type=F32)
+        part = wide[:k] + wide[k : 2 * k]
+        if final:
+            part = jnp.concatenate([part, wide[2 * k : 3 * k] + wide[3 * k :]], axis=0)
+        gram = gram + (part + lax.dot_general(tops, low, dims, preferred_element_type=F32))
+    gram = jnp.concatenate([gram] * (LANES // k), axis=1)
     half = squares.shape[1]
     if final:
         grams[mine] = jnp.concatenate([pack(gram[:k]), pack(gram[k:])], axis=0)
@@ -269,10 +276,13 @@
     row = lax.broadcasted_iota(jnp.int32, (k, LANES), 0)
     lane = lax.broadcasted_iota(jnp.int32, (k, LANES), 1)
     inverse = inverse_factor(gram / count + jnp.where(row == lane, EPSILON, 0.0))
+    top, rest = halves(inverse)
+    stacked = jnp.concatenate([top, rest], axis=0)
     for at in range(pieces):
-        dirs_ref[:, at * chunk : (at + 1) * chunk] = jnp.dot(
-            inverse, shrunk[at], precision=HIGH, preferred_element_type=F32
-        )
+        high, low = shrunk[at]
+        wide = jnp.dot(stacked, high, preferred_element_type=F32)
+        last = jnp.dot(top, low, preferred_element_type=F32)
+        dirs_ref[:, at * chunk : (at + 1) * chunk] = wide[:k] + (wide[k:] + last)
     if final:
         strength = jnp.sum(cross_gram[:, :k] * inverse, axis=1, keepdims=True)
         outs[1][...] = jnp.broadcast_to(strength, (k, LANES))

time: 268 us -> 260 us (0.970)
  Pallas kernels: 260 us -> 253 us
    pallas_call x4, Pallas kernels: 144 us -> 136 us  [orth_step(): pl.pallas_call(functools.partial(orth_kernel, axis, parts, other_axis, ot...]
where the time goes in v2:
time: 260 us; the launch traced here: 259 us
  Pallas kernels  253 us (97%)
  local copies, waits for them, and re-layouts  2.9 us (1%)
  other arithmetic  2.63 us (1%)
    pallas_call x4, Pallas kernels, orth_step(): pl.pallas_call(functools.partial(orth_kernel, axis, parts, other_axis, ot...  136 us
    pallas_call x2, Pallas kernels, left_pass(): pl.pallas_call(functools.partial(left_kernel, chunk), out_shape=jax.Shape...  43.4 us
    pallas_call x2, Pallas kernels, right_pass(): pl.pallas_call(right_kernel, out_shape=jax.ShapeDtypeStruct((cols // chun...  39.3 us
    pallas_call x1, Pallas kernels, deflate(): pl.pallas_call(deflate_kernel, out_shape=jax.ShapeDtypeStruct((rows, cols...  34.1 us

profile of v2, /device:TPU:0, one launch (start us, length us, event | category | flops | bytes accessed | tf_op | source)
XLA Modules:
  0.0 259.2 jit_solution(10095620764896862750)
XLA Ops:
  0.6 0.7 convert_multiply_fusion
  1.3 0.7 broadcast_in_dim.13.thr_ref
  2.0 21.7 %left_pass.2.part_ref = f32[8,32,512]{2,1,0:T(8,128)} custom-call(f32[32,3072]{1,0:T(8,128)} %dirs_ref.1, f32[4096,3072]{1,0:T(8,128)} %cross_ref.9), custom_call_target="tpu_custom_call" | custom-call | tf_op jit(solution)/shard_map/left_pass/pallas_call | solution.py:54
  23.7 38.8 %orth_0.1.dirs_ref = f32[32,4096]{1,0:T(8,128)} custom-call(f32[8,32,512]{2,1,0:T(8,128)} %left_pass.2.part_ref, f32[32,128]{1,0:T(8,128)} %broadcast_in_dim.13.thr_ref), custom_call_target="tpu_custom_call" | custom-call | tf_op jit(solution)/shard_map/orth_0/pallas_call | solution.py:302
  62.5 19.7 %right_pass.2.part_ref = f32[4,32,768]{2,1,0:T(8,128)} custom-call(f32[32,4096]{1,0:T(8,128)} %orth_0.1.dirs_ref, f32[4096,3072]{1,0:T(8,128)} %cross_ref.9), custom_call_target="tpu_custom_call" | custom-call | tf_op jit(solution)/shard_map/right_pass/pallas_call | solution.py:88
  82.2 0.7 broadcast_in_dim.15.thr_ref
  82.9 32.5 %orth_1.1.dirs_ref = f32[32,3072]{1,0:T(8,128)} custom-call(f32[4,32,768]{2,1,0:T(8,128)} %right_pass.2.part_ref, f32[32,128]{1,0:T(8,128)} %broadcast_in_dim.15.thr_ref), custom_call_target="tpu_custom_call" | custom-call | tf_op jit(solution)/shard_map/orth_1/pallas_call | solution.py:302
  115.3 21.7 %left_pass.3.part_ref = f32[8,32,512]{2,1,0:T(8,128)} custom-call(f32[32,3072]{1,0:T(8,128)} %orth_1.1.dirs_ref, f32[4096,3072]{1,0:T(8,128)} %cross_ref.9), custom_call_target="tpu_custom_call" | custom-call | tf_op jit(solution)/shard_map/left_pass/pallas_call | solution.py:54
  137.0 36.0 %orth_2.1.dirs_ref.left_ref = f32[32,4096]{1,0:T(8,128)} custom-call(f32[8,32,512]{2,1,0:T(8,128)} %left_pass.3.part_ref, f32[32,128]{1,0:T(8,128)} %broadcast_in_dim.13.thr_ref), custom_call_target="tpu_custom_call" | custom-call | tf_op jit(solution)/shard_map/orth_2/pallas_call | solution.py:302
  173.1 19.7 %right_pass.3.part_ref = f32[4,32,768]{2,1,0:T(8,128)} custom-call(f32[32,4096]{1,0:T(8,128)} %orth_2.1.dirs_ref.left_ref, f32[4096,3072]{1,0:T(8,128)} %cross_ref.9), custom_call_target="tpu_custom_call" | custom-call | tf_op jit(solution)/shard_map/right_pass/pallas_call | solution.py:88
  192.7 28.9 %orth_3.1 = (f32[32,3072]{1,0:T(8,128)}, f32[32,128]{1,0:T(8,128)}) custom-call(f32[4,32,768]{2,1,0:T(8,128)} %right_pass.3.part_ref, f32[32,128]{1,0:T(8,128)} %broadcast_in_dim.15.thr_ref), custom_call_target="tpu_custom_call" | custom-call | tf_op jit(solution)/shard_map/orth_3/pallas_call | solution.py:302
  221.6 1.3 broadcast_multiply_fusion.scale_ref
  222.9 0.0 copy-start.2
  222.9 0.0 copy-start
  222.9 0.0 copy-start.1
  222.9 34.1 %deflate.1 = f32[4096,3072]{1,0:T(8,128)} custom-call(f32[32,4096]{1,0:T(8,128)} %orth_2.1.dirs_ref.left_ref, f32[32,128]{1,0:T(8,128)} %broadcast_multiply_fusion.scale_ref, f32[32,3072]{1,0:T(8,128)} %get-tuple-element.16.right_ref, f32[4096,3072]{1,0:T(8,128)} %cross_ref.9), custom_call_target="tpu_custom_call" | custom-call | tf_op jit(solution)/shard_map/deflate/pallas_call | solution.py:124
  257.0 0.0 copy-done.2
  257.0 0.6 fusion
  257.7 0.0 copy-done
  257.7 0.8 copy.9
  258.5 0.0 copy-done.1
  258.5 0.7 copy.10
  (1 shorter events, 0.0 us)
Async XLA Ops:
  222.9 34.1 %copy-start.2 = (f32[32,128]{1,0:T(8,128)S(1)}, f32[32,128]{1,0:T(8,128)}, u32[]{:S(2)}) copy-start(f32[32,128]{1,0:T(8,128)} %get-tuple-element.6) | copy-start | bytes 49156
  222.9 34.7 %copy-start = (f32[32,4096]{1,0:T(8,128)S(1)}, f32[32,4096]{1,0:T(8,128)}, u32[]{:S(2)}) copy-start(f32[32,4096]{1,0:T(8,128)} %orth_2.1.dirs_ref.left_ref) | copy-start | bytes 1572868
  222.9 35.5 %copy-start.1 = (f32[32,3072]{1,0:T(8,128)S(1)}, f32[32,3072]{1,0:T(8,128)}, u32[]{:S(2)}) copy-start(f32[32,3072]{1,0:T(8,128)} %get-tuple-element.16.right_ref) | copy-start | bytes 1179652
